TPU v7x, 32 devices: a whole 2x2x4 slice. The times are simulated.
32 devices in a mesh: grp: 2 (over y), seq: 4 (over z), ch: 2 (over x), sub: 2 (over core).
Axes of the slice: x: 2, y: 2, z: 4, core: 2. Of those that a mesh axis runs over, the one named last changes fastest.
Arguments:
- token_ids: int32 [2048], P(('grp', 'seq')), parts along dimension 0, may hold values from 0 to 511
- residual_in: bfloat16 [2048, 4096], P(('grp', 'seq'), ('ch', 'sub')), parts along dimension 0, may hold values from -6 to 6
- embedding: bfloat16 [512, 4096], P(None, ('ch', 'sub')), may hold values from -6 to 6
- in_weight: bfloat16 [4096, 3, 2048], P('seq', None, ('ch', 'sub')), may hold values from -0.09375 to 0.09375
- short_filter: float32 [3, 3, 2048], P(None, None, ('ch', 'sub')), may hold values from -3 to 3
- decay_rate: float32 [16, 2048], P(None, ('ch', 'sub')), may hold values from 1e-05 to 0.05
- residue: float32 [16, 2048], P(None, ('ch', 'sub')), may hold values from -0.24 to 0.24
- skip: float32 [2048], P(('ch', 'sub')), may hold values from -4 to 4
Outputs:
- mixed_out: bfloat16 [2048, 2048], P(('grp', 'seq'), ('ch', 'sub')), parts along dimension 0
There are 2 independent parts, one for each index of `grp`. A program takes and returns all parts, laid end to end along the dimension named above; an argument that names none is the same for every part. Nothing has to cross between parts.
All inputs are finite; a program needn't handle non-finite values.
Results may differ from a plain program's by a relative error of at most 0.0095.
Values may be sent and summed in bfloat16 or wider, within the bound.
A program may use at most 64 MiB of HBM per device.

v0:
```python
import jax
import jax.numpy as jnp
from jax import lax
from jax.sharding import PartitionSpec as P

PRECISE = lax.Precision.HIGHEST
TWO_PI = 6.283185307179586


def shifted(x, axis, by):
    peers = lax.axis_size(axis)
    pairs = [(i, i + by) for i in range(peers) if 0 <= i + by < peers]
    return lax.ppermute(x, axis, pairs)


def swapped(value, axis, apart):
    mask = 2**apart
    pairs = [(source, source ^ mask) for source in range(lax.axis_size(axis))]
    return lax.ppermute(value, axis, pairs)


def reversed_bits(number, bit_count):
    result = jnp.zeros_like(number)
    for section_bit in range(bit_count):
        result = result + (number >> section_bit & 1) * (1 << bit_count - 1 - section_bit)
    return result


def angle_table(left_idx, right_idx, period):
    wrapped = left_idx[:, None] * right_idx[None, :] % period
    return TWO_PI * wrapped.astype(jnp.float32) / period


def complex_mix(mat_re, mat_im, data_re, data_im):
    real_part = jnp.einsum("kr,rjc->kjc", mat_re, data_re, precision=PRECISE) - jnp.einsum(
        "kr,rjc->kjc", mat_im, data_im, precision=PRECISE
    )
    imag_part = jnp.einsum("kr,rjc->kjc", mat_re, data_im, precision=PRECISE) + jnp.einsum(
        "kr,rjc->kjc", mat_im, data_re, precision=PRECISE
    )
    return (real_part, imag_part)


def complex_dot(mat_re, mat_im, data_re, data_im):
    real_part = jnp.dot(mat_re, data_re, precision=PRECISE) - jnp.dot(
        mat_im, data_im, precision=PRECISE
    )
    imag_part = jnp.dot(mat_re, data_im, precision=PRECISE) + jnp.dot(
        mat_im, data_re, precision=PRECISE
    )
    return (real_part, imag_part)


def shards(token_ids, residual_in, embedding, in_weight, short_filter, decay_rate, residue, skip):
    tok_rows = residual_in.shape[0]
    vocab_size = embedding.shape[0]
    channels = skip.shape[0]
    seq_parts = lax.axis_size("seq")
    bit_count = seq_parts.bit_length() - 1
    my_index = lax.axis_index("seq")
    length = tok_rows * seq_parts
    padded_len = 2 * length
    group_rows = tok_rows // seq_parts
    onehot = (token_ids[:, None] == jnp.arange(vocab_size, dtype=jnp.int32)[None, :]).astype(
        jnp.bfloat16
    )
    embedded = jnp.dot(onehot, embedding, preferred_element_type=jnp.float32)
    inputs = (residual_in.astype(jnp.float32) + embedded).astype(jnp.bfloat16)
    features = lax.all_gather(inputs, ("ch", "sub"), axis=1, tiled=True)
    piece_rows = lax.all_gather(in_weight, "seq", axis=0, tiled=True)
    flat_piece = piece_rows.reshape(piece_rows.shape[0], 3 * channels)
    projected = jnp.dot(features, flat_piece, preferred_element_type=jnp.float32)
    projected = projected.astype(jnp.bfloat16).reshape(tok_rows, 3, channels)
    rim_rows = shifted(projected[tok_rows - 2 :], "seq", 1)
    extended = jnp.concatenate([rim_rows, projected], axis=0).astype(jnp.float32)
    mixed_in = (
        short_filter[0] * extended[2:]
        + short_filter[1] * extended[1:-1]
        + short_filter[2] * extended[:-2]
    )
    query_gate = mixed_in[:, 0]
    product = (mixed_in[:, 1] * mixed_in[:, 2]).astype(jnp.bfloat16)
    local_pos = jnp.arange(tok_rows, dtype=jnp.int32)
    sources = jnp.arange(seq_parts, dtype=jnp.int32)
    within_rows = my_index * group_rows + jnp.arange(group_rows, dtype=jnp.int32)
    block_pos = sources[:, None] * tok_rows + within_rows[None, :]
    block_angle = TWO_PI * block_pos.astype(jnp.float32) / padded_len
    pos_angle = TWO_PI * (my_index * tok_rows + local_pos).astype(jnp.float32) / padded_len
    values = product.astype(jnp.float32)
    state_re = jnp.concatenate([values, values * jnp.cos(pos_angle)[:, None]], -1)
    state_im = jnp.concatenate([jnp.zeros_like(values), -values * jnp.sin(pos_angle)[:, None]], -1)
    state_now = jnp.stack([state_re, state_im])
    for section_bit in range(bit_count - 1, -1, -1):
        half_span = 1 << section_bit
        partner = swapped(state_now.astype(jnp.bfloat16), "seq", section_bit).astype(
            state_now.dtype
        )
        upper_half = my_index >> section_bit & 1 == 1
        phase_now = TWO_PI * (my_index % half_span).astype(jnp.float32) / (2 * half_span)
        difference = partner - state_now
        rot_re = difference[0] * jnp.cos(phase_now) + difference[1] * jnp.sin(phase_now)
        rot_im = difference[1] * jnp.cos(phase_now) - difference[0] * jnp.sin(phase_now)
        state_now = jnp.where(upper_half, jnp.stack([rot_re, rot_im]), state_now + partner)
    own_freq = reversed_bits(my_index, bit_count)
    holders = reversed_bits(sources, bit_count)
    twist_angle = TWO_PI * (local_pos * own_freq % length).astype(jnp.float32) / length
    twist_re = jnp.cos(twist_angle)[:, None]
    twist_im = -jnp.sin(twist_angle)[:, None]
    spec_re = state_now[0] * twist_re - state_now[1] * twist_im
    spec_im = state_now[0] * twist_im + state_now[1] * twist_re
    kernel_table = angle_table(local_pos, local_pos, tok_rows)
    dft_re = jnp.cos(kernel_table)
    dft_im = -jnp.sin(kernel_table)
    spec_re, spec_im = complex_dot(dft_re, dft_im, spec_re, spec_im)
    parity = (jnp.arange(2 * channels, dtype=jnp.int32) >= channels).astype(jnp.int32)
    full_freq = 2 * (own_freq + seq_parts * local_pos)[:, None] + parity[None, :]
    freq_angle = TWO_PI * full_freq.astype(jnp.float32) / padded_len
    half_sine = jnp.sin(0.5 * freq_angle)
    sine_full = jnp.sin(freq_angle)
    sign_flip = 1.0 - 2.0 * parity.astype(jnp.float32)
    rates_both = jnp.concatenate([decay_rate, decay_rate], -1)
    residues_both = jnp.concatenate([residue, residue], -1)
    filt_re = jnp.zeros_like(spec_re)
    filt_im = jnp.zeros_like(spec_re)
    for mode_index in range(rates_both.shape[0]):
        rate_now = rates_both[mode_index]
        decay_now = jnp.exp(-rate_now)
        numerator = residues_both[mode_index] * (1.0 - sign_flip * jnp.exp(-rate_now * length))
        denom_re = -jnp.expm1(-rate_now) + 2.0 * decay_now * half_sine * half_sine
        denom_im = decay_now * sine_full
        scaled = numerator / (denom_re * denom_re + denom_im * denom_im)
        filt_re = filt_re + scaled * denom_re
        filt_im = filt_im - scaled * denom_im
    prod_re = spec_re * filt_re - spec_im * filt_im
    prod_im = spec_re * filt_im + spec_im * filt_re
    inv_re, inv_im = complex_dot(dft_re, -dft_im, prod_re, prod_im)
    back_re = inv_re * twist_re + inv_im * twist_im
    back_im = inv_im * twist_re - inv_re * twist_im
    returned = lax.all_to_all(
        jnp.stack([back_re, back_im]).reshape(2, 1, tok_rows, 2 * channels).astype(jnp.bfloat16),
        "seq",
        split_axis=2,
        concat_axis=1,
        tiled=True,
    ).astype(jnp.float32)
    inverse_angle = angle_table(sources, holders, seq_parts)
    block_re, block_im = complex_mix(
        jnp.cos(inverse_angle), jnp.sin(inverse_angle), returned[0], returned[1]
    )
    conv_blocks = (
        block_re[..., :channels]
        + jnp.cos(block_angle)[:, :, None] * block_re[..., channels:]
        - jnp.sin(block_angle)[:, :, None] * block_im[..., channels:]
    )
    conv_blocks = conv_blocks / padded_len
    conv_rows = lax.all_to_all(conv_blocks, "seq", split_axis=0, concat_axis=1, tiled=True)[0]
    mixed_out = (query_gate * (conv_rows + skip * product.astype(jnp.float32))).astype(jnp.bfloat16)
    return mixed_out


def solution(mesh):
    return jax.shard_map(
        shards,
        mesh=mesh,
        in_specs=(
            P(("grp", "seq")),
            P(("grp", "seq"), ("ch", "sub")),
            P(None, ("ch", "sub")),
            P("seq", None, ("ch", "sub")),
            P(None, None, ("ch", "sub")),
            P(None, ("ch", "sub")),
            P(None, ("ch", "sub")),
            P(("ch", "sub")),
        ),
        out_specs=P(("grp", "seq"), ("ch", "sub")),
        check_vma=False,
    )
```

profile of v0, /device:TPU:0, one launch (start us, length us, event | category | flops | bytes accessed | tf_op | source)
XLA Modules:
  0.0 444.1 jit_solution(15915545846270894361)
XLA Ops:
  6.5 1.2 copy-done
  7.8 2.3 fusion.5
  10.2 4.7 %copy.55 = bf16[1024,3,512]{0,2,1:T(8,128)(2,1)} copy(bf16[1024,3,512]{2,0,1:T(8,128)(2,1)} %param.11) | data formatting | bytes 6291456 | tf_op args[3]
  15.6 20.0 %all-gather.3.cloned.1.call-done = bf16[256,4096]{1,0:T(8,128)(2,1)} async-done(((bf16[256,1024]{1,0:T(8,128)(2,1)}), bf16[256,4096]{1,0:T(8,128)(2,1)}) %all-gather.3.cloned.1.call-update) | async-done | bytes 2097168 | tf_op jit(solution)/shard_map/all_gather | solution.py:69
  35.6 219.8 %all-gather.5.cloned.1.call-done = bf16[4096,3,512]{0,2,1:T(8,128)(2,1)} async-done(((bf16[1024,3,512]{0,2,1:T(8,128)(2,1)}), bf16[4096,3,512]{0,2,1:T(8,128)(2,1)}) %all-gather.5.cloned.1.call-update) | async-done | bytes 12582928 | tf_op jit(solution)/shard_map/all_gather | solution.py:70
  255.4 8.7 %convolution_convert_fusion = bf16[256,1536]{1,0:T(8,128)(2,1)S(1)} fusion(bf16[256,4096]{1,0:T(8,128)(2,1)} %all-gather.3.cloned.1.call-done, bf16[4096,1536]{0,1:T(8,128)(2,1)} %bitcast.208), kind=kOutput, calls=%fused_computation.4 | convolution fusion | flops 3221618688 | bytes 15466496 | tf_op jit(solution)/shard_map/dot_general | solution.py:72
  264.0 1.5 collective-permute-start
  267.7 0.8 copy-done.3
  268.7 1.3 fusion.4
  269.9 3.5 collective-permute-start.1
  274.4 0.8 constant_dynamic-update-slice_fusion
  275.8 42.2 %collective-permute-done.1 = bf16[2,256,1024]{2,1,0:T(8,128)(2,1)S(1)} collective-permute-done((bf16[2,256,1024]{2,1,0:T(8,128)(2,1)}, bf16[2,256,1024]{2,1,0:T(8,128)(2,1)S(1)}, u32[]{:S(2)}, u32[]{:S(2)}) %collective-permute-start.1) | collective-permute-done | bytes 1048608 | tf_op jit(solution)/shard_map/ppermute | solution.py:19
  319.3 3.2 fusion.171
  323.5 22.9 %collective-permute-done.2 = bf16[2,256,1024]{2,1,0:T(8,128)(2,1)S(1)} collective-permute-done((bf16[2,256,1024]{2,1,0:T(8,128)(2,1)}, bf16[2,256,1024]{2,1,0:T(8,128)(2,1)S(1)}, u32[]{:S(2)}, u32[]{:S(2)}) %collective-permute-start.2) | collective-permute-done | bytes 1048608 | tf_op jit(solution)/shard_map/ppermute | solution.py:19
  347.5 2.2 fusion.72
  349.7 2.2 fusion.70
  352.0 2.2 convolution_subtract_fusion.2
  354.3 18.1 %multiply_add_fusion = (f32[256,1024]{1,0:T(8,128)S(1)}, f32[256,1024]{1,0:T(8,128)S(1)}, f32[256,1024]{1,0:T(8,128)S(1)}, f32[256,1024]{1,0:T(8,128)S(1)}) fusion(f32[256,1024]{1,0:T(8,128)S(1)} %convolution_subtract_fusion.2, f32[1024]{0:T(1024)S(1)} %bitcast.145, f32[1024]{0:T(1024)S(1)} %bitcast.146, f32[1024]{0:T(1024)S(1)} %bitcast.191, ...), kind=kOutput, calls=%fused_computation.59 | convolution fusion | flops 859242496 | bytes 8657920 | tf_op jit(solution)/shard_map/dot_general | solution.py:48
  372.3 2.0 fusion.66
  374.8 2.0 fusion.68
  376.8 2.2 convolution_add_fusion.1
  379.0 2.3 fusion.38
  381.5 2.1 copy.59
  383.6 4.3 all-to-all-start
  388.2 23.8 %all-to-all-done = bf16[2,1,256,1024]{3,0,1,2:T(2,128)(2,1)S(1)} async-done(((bf16[2,1,256,1024]{3,0,1,2:T(2,128)(2,1)}), bf16[2,1,256,1024]{3,0,1,2:T(2,128)(2,1)S(1)}, u32[]{:S(2)}, u32[]{:S(2)}) %all-to-all-start) | async-done | bytes 1048608 | tf_op jit(solution)/shard_map/all_to_all | solution.py:139
  412.1 1.5 fusion.175
  413.7 1.1 fusion.52
  414.8 1.1 fusion.50
  416.0 1.1 fusion.47
  417.1 1.1 convolution_subtract_fusion
  418.8 16.5 %all_to_all.8 = f32[4,64,512]{2,1,0:T(8,128)S(1)} all-to-all(f32[4,64,512]{2,1,0:T(8,128)S(1)} %copy.68), channel_id=1, replica_groups=mesh['grp'=2,'seq'=4,'ch'=2,'sub'=2] {'seq'}, dimensions={0} | all-to-all | bytes 1048576 | tf_op jit(solution)/shard_map/all_to_all | solution.py:156
  435.2 1.8 fusion.46
  (74 shorter events, 9.6 us)
Async XLA Ops:
  6.5 1.2 copy-start
  6.5 29.0 %all-gather.3.cloned.1.call-start = ((), (), s32[]{:S(2)}) async-start(), calls=%async_computation.2 | async-start | bytes 2621440 | tf_op jit(solution)/shard_map/all_gather | solution.py:69
  10.1 245.2 %all-gather.5.cloned.1.call-start = ((), (), s32[]{:S(2)}) async-start(), calls=%async_computation.3 | async-start | bytes 15728640 | tf_op jit(solution)/shard_map/all_gather | solution.py:70
  14.9 0.7 copy-start.6
  264.0 2.6 collective-permute-start
  267.4 1.2 copy-start.3
  268.6 49.7 %copy-start.2 = (f32[1,256,1024]{2,1,0:T(8,128)}, f32[1,256,1024]{2,1,0:T(8,128)S(1)}, u32[]{:S(2)}) copy-start(f32[1,256,1024]{2,1,0:T(8,128)S(1)} %maximum_bitcast_fusion) | copy-start | bytes 3145732
  268.6 5.0 %copy-start.5 = (f32[16,512]{1,0:T(8,128)S(1)}, f32[16,512]{1,0:T(8,128)}, u32[]{:S(2)}) copy-start(f32[16,512]{1,0:T(8,128)} %param.14) | copy-start | bytes 98308
  269.9 48.1 %collective-permute-start.1 = (bf16[2,256,1024]{2,1,0:T(8,128)(2,1)}, bf16[2,256,1024]{2,1,0:T(8,128)(2,1)S(1)}, u32[]{:S(2)}, u32[]{:S(2)}) collective-permute-start(bf16[2,256,1024]{2,1,0:T(8,128)(2,1)} %fusion.4), channel_id=1, source_target_pairs={{0,8},{4,12},{8,0},{12,4},{1,9},{5,13},{9,1},{13,5},{2,10},{6,14},... | collective-permute-start | bytes 3145736 | tf_op jit(solution)/shard_map/ppermute | solution.py:19
  318.0 1.0 copy-start.4
  322.5 23.9 %collective-permute-start.2 = (bf16[2,256,1024]{2,1,0:T(8,128)(2,1)}, bf16[2,256,1024]{2,1,0:T(8,128)(2,1)S(1)}, u32[]{:S(2)}, u32[]{:S(2)}) collective-permute-start(bf16[2,256,1024]{2,1,0:T(8,128)(2,1)} %get-tuple-element.8), channel_id=1, source_target_pairs={{0,4},{4,0},{8,12},{12,8},{1,5},{5,1},{9,13},{13,9},{2,6},{6,2},{1... | collective-permute-start | bytes 3145736 | tf_op jit(solution)/shard_map/ppermute | solution.py:19
  351.9 2.3 copy-start.7
  351.9 2.3 copy-start.8
  351.9 2.3 copy-start.9
  351.9 2.3 copy-start.10
  351.9 2.3 copy-start.11
  351.9 2.3 copy-start.12
  351.9 2.3 copy-start.13
  352.0 2.3 copy-start.15
  383.6 28.5 %all-to-all-start = ((bf16[2,1,256,1024]{3,0,1,2:T(2,128)(2,1)}), bf16[2,1,256,1024]{3,0,1,2:T(2,128)(2,1)S(1)}, u32[]{:S(2)}, u32[]{:S(2)}) async-start(bf16[2,1,256,1024]{3,0,1,2:T(2,128)(2,1)} %copy.59), calls=%async_computation | async-start | bytes 2097152 | tf_op jit(solution)/shard_map/all_to_all | solution.py:139
  418.2 17.0 %copy-start.14 = (f32[512]{0:T(512)S(1)}, f32[512]{0:T(512)}, u32[]{:S(2)}) copy-start(f32[512]{0:T(512)} %param.15) | copy-start | bytes 6148
  418.2 18.8 %copy-start.1 = (bf16[512,1024]{1,0:T(8,128)(2,1)S(1)}, bf16[512,1024]{1,0:T(8,128)(2,1)}, u32[]{:S(2)}) copy-start(bf16[512,1024]{1,0:T(8,128)(2,1)} %param.10) | copy-start | bytes 3145732
Sparse Core Ops, SparseCore 0:
  10.3 25.2 all-gather.2
  37.1 218.1 all-gather.4
where the time goes:
time: 448 us; the launch traced here: 444 us
  waiting for transfers between devices  329 us (73%)
  matrix products  48.5 us (11%)
  blocking collectives  16.5 us (4%)
  local copies, waits for them, and re-layouts  14.6 us (3%)
  between operations  14.2 us (3%)
  other arithmetic  11.7 us (3%)
  starting transfers between devices  9.35 us (2%)
    all_gather x1, waiting for transfers between devices, shards(): piece_rows = lax.all_gather(in_weight, 'seq', axis=0, tiled=True)  220 us
    ppermute x2, waiting for transfers between devices, swapped(): return lax.ppermute(value, axis, pairs)  65.1 us
    all_to_all x1, waiting for transfers between devices, shards(): lax.all_to_all(jnp.stack([back_re, back_im]).reshape(2, 1, tok_rows, 2 *...  23.8 us
    dot_general x2, matrix products, complex_dot(): jnp.dot(mat_im, data_re, precision=PRECISE)  20.3 us
    all_gather x1, waiting for transfers between devices, shards(): features = lax.all_gather(inputs, ('ch', 'sub'), axis=1, tiled=True)  20 us
    all_to_all x1, blocking collectives, shards(): lax.all_to_all(conv_blocks, 'seq', split_axis=0, concat_axis=1, tiled=True)  16.5 us
    unnamed x37, local copies, waits for them, and re-layouts  9.23 us
  transfers between devices with their start and end apart: 6, of which 6 were waited for; matrix products, arithmetic and copies ran while one was open for 2% of the time, Pallas kernels for 0%

commit v1 on v0

--- a/solution.py
+++ b/solution.py
@@ -1,3 +1,4 @@
+import functools
 import jax
 import jax.numpy as jnp
 from jax import lax
@@ -5,6 +6,32 @@
 
 PRECISE = lax.Precision.HIGHEST
 TWO_PI = 6.283185307179586
+
+
+def _review_copies(message, comm_axis, d_out, array_dim):
+    top = lax.axis_size(comm_axis)
+    val = lax.axis_index(comm_axis)
+    left_arr, mixed_arr = (top, val)
+    near = message.shape[d_out] // left_arr
+    outer = list(message.shape)
+    outer[d_out] = near
+    back = outer[array_dim]
+    outer[array_dim] = back * left_arr
+    block_out = jnp.zeros(outer, message.dtype)
+    for it in range(left_arr):
+        taken_in = lax.dynamic_slice_in_dim(message, (mixed_arr ^ it) * near, near, axis=d_out)
+        if it:
+            piece_now = range(left_arr)
+            x_new = map(lambda ii: (ii, ii ^ it), piece_now)
+            a_now = list(x_new)
+            taken_in = lax.ppermute(taken_in, comm_axis, a_now)
+        block_out = lax.dynamic_update_slice_in_dim(
+            block_out, taken_in, (mixed_arr ^ it) * back, axis=array_dim
+        )
+    return block_out
+
+
+_group_lines = functools.partial(_review_copies, comm_axis="seq", d_out=2, array_dim=1)
 
 
 def shifted(x, axis, by):
@@ -136,12 +163,8 @@
     inv_re, inv_im = complex_dot(dft_re, -dft_im, prod_re, prod_im)
     back_re = inv_re * twist_re + inv_im * twist_im
     back_im = inv_im * twist_re - inv_re * twist_im
-    returned = lax.all_to_all(
-        jnp.stack([back_re, back_im]).reshape(2, 1, tok_rows, 2 * channels).astype(jnp.bfloat16),
-        "seq",
-        split_axis=2,
-        concat_axis=1,
-        tiled=True,
+    returned = _group_lines(
+        jnp.stack([back_re, back_im]).reshape(2, 1, tok_rows, 2 * channels).astype(jnp.bfloat16)
     ).astype(jnp.float32)
     inverse_angle = angle_table(sources, holders, seq_parts)
     block_re, block_im = complex_mix(

time: 448 us -> 444 us (level)
  waiting for transfers between devices: 329 us -> 313 us
  local copies, waits for them, and re-layouts: 14.6 us -> 27.7 us
    all_to_all x1 -> x0, waiting for transfers between devices: 23.8 us -> none  [shards(): lax.all_to_all(jnp.stack([back_re, back_im]).reshape(2, 1, tok_rows, 2 *...]
    dynamic_update_slice x0 -> x4, local copies, waits for them, and re-layouts: none -> 14.1 us  [_review_copies(): lax.dynamic_update_slice_in_dim(block_out, taken_in, (mixed_arr ^ it) * b...]
    ppermute x0 -> x3, waiting for transfers between devices: none -> 8.22 us  [_review_copies(): taken_in = lax.ppermute(taken_in, comm_axis, a_now)]
    unnamed x37 -> x39, local copies, waits for them, and re-layouts: 9.23 us -> 8.91 us
  transfers between devices with their start and end apart: 6 -> 8, of which waited for: 6 -> 7; matrix products, arithmetic and copies ran while one was open for 2% -> 5% of each run, Pallas kernels for 0% -> 0%
where the time goes in v1:
time: 444 us; the launch traced here: 440 us
  waiting for transfers between devices  313 us (70%)
  matrix products  48.7 us (11%)
  local copies, waits for them, and re-layouts  27.7 us (6%)
  blocking collectives  14.7 us (3%)
  between operations  14.3 us (3%)
  other arithmetic  12.7 us (3%)
  starting transfers between devices  9.46 us (2%)
    all_gather x1, waiting for transfers between devices, shards(): piece_rows = lax.all_gather(in_weight, 'seq', axis=0, tiled=True)  220 us
    ppermute x2, waiting for transfers between devices, swapped(): return lax.ppermute(value, axis, pairs)  64.1 us
    dot_general x2, matrix products, complex_dot(): jnp.dot(mat_im, data_re, precision=PRECISE)  20.5 us
    all_gather x1, waiting for transfers between devices, shards(): features = lax.all_gather(inputs, ('ch', 'sub'), axis=1, tiled=True)  20 us
    all_to_all x1, blocking collectives, shards(): lax.all_to_all(conv_blocks, 'seq', split_axis=0, concat_axis=1, tiled=True)  14.7 us
    dynamic_update_slice x4, local copies, waits for them, and re-layouts, _review_copies(): lax.dynamic_update_slice_in_dim(block_out, taken_in, (mixed_arr ^ it) * b...  14.1 us
    unnamed x39, local copies, waits for them, and re-layouts  8.91 us
  transfers between devices with their start and end apart: 8, of which 7 were waited for; matrix products, arithmetic and copies ran while one was open for 5% of the time, Pallas kernels for 0%

profile of v1, /device:TPU:0, one launch (start us, length us, event | category | flops | bytes accessed | tf_op | source)
XLA Modules:
  0.0 440.2 jit_solution(7021209127345861695)
XLA Ops:
  6.5 1.2 copy-done
  7.8 2.3 fusion.5
  10.2 4.7 %copy.34 = bf16[1024,3,512]{0,2,1:T(8,128)(2,1)} copy(bf16[1024,3,512]{2,0,1:T(8,128)(2,1)} %param.11) | data formatting | bytes 6291456 | tf_op args[3]
  15.6 20.0 %all-gather.3.cloned.1.call-done = bf16[256,4096]{1,0:T(8,128)(2,1)} async-done(((bf16[256,1024]{1,0:T(8,128)(2,1)}), bf16[256,4096]{1,0:T(8,128)(2,1)}) %all-gather.3.cloned.1.call-update) | async-done | bytes 2097168 | tf_op jit(solution)/shard_map/all_gather | solution.py:96
  35.6 219.8 %all-gather.5.cloned.1.call-done = bf16[4096,3,512]{0,2,1:T(8,128)(2,1)} async-done(((bf16[1024,3,512]{0,2,1:T(8,128)(2,1)}), bf16[4096,3,512]{0,2,1:T(8,128)(2,1)}) %all-gather.5.cloned.1.call-update) | async-done | bytes 12582928 | tf_op jit(solution)/shard_map/all_gather | solution.py:97
  255.4 8.7 %convolution_convert_fusion = bf16[256,1536]{1,0:T(8,128)(2,1)S(1)} fusion(bf16[256,4096]{1,0:T(8,128)(2,1)} %all-gather.3.cloned.1.call-done, bf16[4096,1536]{0,1:T(8,128)(2,1)} %bitcast.210), kind=kOutput, calls=%fused_computation.4 | convolution fusion | flops 3221618688 | bytes 15466496 | tf_op jit(solution)/shard_map/dot_general | solution.py:99
  264.0 1.5 collective-permute-start
  268.7 1.3 fusion.4
  269.9 3.5 collective-permute-start.1
  277.0 41.1 %collective-permute-done.1 = bf16[2,256,1024]{2,1,0:T(8,128)(2,1)S(1)} collective-permute-done((bf16[2,256,1024]{2,1,0:T(8,128)(2,1)}, bf16[2,256,1024]{2,1,0:T(8,128)(2,1)S(1)}, u32[]{:S(2)}, u32[]{:S(2)}) %collective-permute-start.1) | collective-permute-done | bytes 1048608 | tf_op jit(solution)/shard_map/ppermute | solution.py:46
  319.3 3.2 fusion.167
  323.4 23.0 %collective-permute-done.2 = bf16[2,256,1024]{2,1,0:T(8,128)(2,1)S(1)} collective-permute-done((bf16[2,256,1024]{2,1,0:T(8,128)(2,1)}, bf16[2,256,1024]{2,1,0:T(8,128)(2,1)S(1)}, u32[]{:S(2)}, u32[]{:S(2)}) %collective-permute-start.2) | collective-permute-done | bytes 1048608 | tf_op jit(solution)/shard_map/ppermute | solution.py:46
  347.5 2.2 fusion.72
  349.7 2.2 fusion.70
  352.0 2.2 convolution_subtract_fusion.2
  354.3 18.3 %multiply_subtract_fusion = (f32[256,1024]{1,0:T(8,128)S(1)}, f32[256,1024]{1,0:T(8,128)S(1)}, f32[256,1024]{1,0:T(8,128)S(1)}, f32[256,1024]{1,0:T(8,128)S(1)}) fusion(f32[256,1024]{1,0:T(8,128)S(1)} %convolution_subtract_fusion.2, f32[1024]{0:T(1024)S(1)} %bitcast.147, f32[1024]{0:T(1024)S(1)} %bitcast.148, f32[1024]{0:T(1024)S(1)} %bitcast.193, ...), kind=kOutput, calls=%fused_computation.67 | convolution fusion | flops 859242496 | bytes 8657920 | tf_op jit(solution)/shard_map/dot_general | solution.py:75
  373.0 2.0 fusion.66
  375.0 2.0 fusion.68
  377.0 2.3 convolution_add_fusion.1
  379.3 2.3 fusion.39
  382.2 3.3 collective-permute-start.4
  387.3 3.5 dynamic_update_slice.12
  390.8 1.3 collective-permute-done.3
  392.1 1.4 copy.39
  393.5 3.5 dynamic_update_slice.13
  397.0 6.9 %collective-permute-done.4 = bf16[2,1,64,1024]{3,2,1,0:T(8,128)(2,1)S(1)} collective-permute-done((bf16[2,1,64,1024]{3,2,1,0:T(8,128)(2,1)S(1)}, bf16[2,1,64,1024]{3,2,1,0:T(8,128)(2,1)S(1)}, u32[]{:S(2)}, u32[]{:S(2)}) %collective-permute-start.4) | collective-permute-done | bytes 262176 | tf_op jit(solution)/shard_map/ppermute | solution.py:27
  404.3 3.5 dynamic_update_slice.14
  408.3 3.5 dynamic_update_slice.15
  411.8 1.0 fusion.49
  414.9 1.1 convolution_subtract_fusion
  416.6 14.7 %all_to_all.4 = f32[4,64,512]{2,1,0:T(8,128)S(1)} all-to-all(f32[4,64,512]{2,1,0:T(8,128)S(1)} %copy.44), channel_id=1, replica_groups=mesh['grp'=2,'seq'=4,'ch'=2,'sub'=2] {'seq'}, dimensions={0} | all-to-all | bytes 1048576 | tf_op jit(solution)/shard_map/all_to_all | solution.py:179
  431.3 1.8 fusion.46
  (87 shorter events, 16.6 us)
Async XLA Ops:
  6.5 1.2 copy-start
  6.5 29.0 %all-gather.3.cloned.1.call-start = ((), (), s32[]{:S(2)}) async-start(), calls=%async_computation.1 | async-start | bytes 2621440 | tf_op jit(solution)/shard_map/all_gather | solution.py:96
  10.1 245.2 %all-gather.5.cloned.1.call-start = ((), (), s32[]{:S(2)}) async-start(), calls=%async_computation.2 | async-start | bytes 15728640 | tf_op jit(solution)/shard_map/all_gather | solution.py:97
  14.9 0.7 copy-start.6
  264.0 2.6 collective-permute-start
  267.4 1.2 copy-start.3
  268.6 49.7 %copy-start.2 = (f32[1,256,1024]{2,1,0:T(8,128)}, f32[1,256,1024]{2,1,0:T(8,128)S(1)}, u32[]{:S(2)}) copy-start(f32[1,256,1024]{2,1,0:T(8,128)S(1)} %maximum_bitcast_fusion) | copy-start | bytes 3145732
  268.7 6.1 %copy-start.5 = (f32[16,512]{1,0:T(8,128)S(1)}, f32[16,512]{1,0:T(8,128)}, u32[]{:S(2)}) copy-start(f32[16,512]{1,0:T(8,128)} %param.14) | copy-start | bytes 98308
  269.9 48.1 %collective-permute-start.1 = (bf16[2,256,1024]{2,1,0:T(8,128)(2,1)}, bf16[2,256,1024]{2,1,0:T(8,128)(2,1)S(1)}, u32[]{:S(2)}, u32[]{:S(2)}) collective-permute-start(bf16[2,256,1024]{2,1,0:T(8,128)(2,1)} %fusion.4), channel_id=1, source_target_pairs={{0,8},{4,12},{8,0},{12,4},{1,9},{5,13},{9,1},{13,5},{2,10},{6,14},... | collective-permute-start | bytes 3145736 | tf_op jit(solution)/shard_map/ppermute | solution.py:46
  318.0 1.0 copy-start.4
  322.5 23.9 %collective-permute-start.2 = (bf16[2,256,1024]{2,1,0:T(8,128)(2,1)}, bf16[2,256,1024]{2,1,0:T(8,128)(2,1)S(1)}, u32[]{:S(2)}, u32[]{:S(2)}) collective-permute-start(bf16[2,256,1024]{2,1,0:T(8,128)(2,1)} %get-tuple-element.8), channel_id=1, source_target_pairs={{0,4},{4,0},{8,12},{12,8},{1,5},{5,1},{9,13},{13,9},{2,6},{6,2},{1... | collective-permute-start | bytes 3145736 | tf_op jit(solution)/shard_map/ppermute | solution.py:46
  351.9 2.3 copy-start.7
  351.9 2.3 copy-start.8
  351.9 2.3 copy-start.9
  351.9 2.3 copy-start.10
  351.9 2.3 copy-start.11
  352.0 2.3 copy-start.12
  352.0 2.3 copy-start.13
  352.0 2.3 copy-start.17
  381.7 4.6 %copy-start.15 = (s32[4]{0:T(128)S(1)}, s32[4]{0:T(128)}, u32[]{:S(2)}) copy-start(s32[4]{0:T(128)} %iota_multiply_fusion) | copy-start | bytes 52
  381.7 4.6 %copy-start.16 = (s32[64]{0:T(128)S(1)}, s32[64]{0:T(128)}, u32[]{:S(2)}) copy-start(s32[64]{0:T(128)} %iota_add_fusion) | copy-start | bytes 772
  381.8 10.3 %collective-permute-start.3 = (bf16[2,1,64,1024]{3,2,1,0:T(8,128)(2,1)S(1)}, bf16[2,1,64,1024]{3,2,1,0:T(8,128)(2,1)}, u32[]{:S(2)}, u32[]{:S(2)}) collective-permute-start(bf16[2,1,64,1024]{3,2,1,0:T(8,128)(2,1)S(1)} %get-tuple-element.20), channel_id=1, source_target_pairs={{0,4},{4,0},{8,12},{12,8},{1,5},{5,1},{9,13},{13,9},{2,6},{6,2},{1... | collective-permute-start | bytes 786440 | tf_op jit(solution)/shard_map/ppermute | solution.py:27
  382.2 21.7 %collective-permute-start.4 = (bf16[2,1,64,1024]{3,2,1,0:T(8,128)(2,1)S(1)}, bf16[2,1,64,1024]{3,2,1,0:T(8,128)(2,1)S(1)}, u32[]{:S(2)}, u32[]{:S(2)}) collective-permute-start(bf16[2,1,64,1024]{3,2,1,0:T(8,128)(2,1)S(1)} %get-tuple-element.21), channel_id=1, source_target_pairs={{0,8},{4,12},{8,0},{12,4},{1,9},{5,13},{9,1},{13,5},{2,10},{6,14},... | collective-permute-start | bytes 786440 | tf_op jit(solution)/shard_map/ppermute | solution.py:27
  385.5 22.3 %collective-permute-start.5 = (bf16[2,1,64,1024]{3,2,1,0:T(8,128)(2,1)S(1)}, bf16[2,1,64,1024]{3,2,1,0:T(8,128)(2,1)S(1)}, u32[]{:S(2)}, u32[]{:S(2)}) collective-permute-start(bf16[2,1,64,1024]{3,2,1,0:T(8,128)(2,1)S(1)} %get-tuple-element.18), channel_id=1, source_target_pairs={{0,12},{4,8},{8,4},{12,0},{1,13},{5,9},{9,5},{13,1},{2,14},{6,10},... | collective-permute-start | bytes 786440 | tf_op jit(solution)/shard_map/ppermute | solution.py:27
  416.0 15.3 %copy-start.14 = (f32[512]{0:T(512)S(1)}, f32[512]{0:T(512)}, u32[]{:S(2)}) copy-start(f32[512]{0:T(512)} %param.15) | copy-start | bytes 6148
  416.0 17.1 %copy-start.1 = (bf16[512,1024]{1,0:T(8,128)(2,1)S(1)}, bf16[512,1024]{1,0:T(8,128)(2,1)}, u32[]{:S(2)}) copy-start(bf16[512,1024]{1,0:T(8,128)(2,1)} %param.10) | copy-start | bytes 3145732
Sparse Core Ops, SparseCore 0:
  10.3 25.2 all-gather.2
  37.1 218.1 all-gather.4
